TPU v7x, 32 devices: a whole 2x2x4 slice. The times are simulated.
32 devices in a mesh: px: 8 (over z, x), py: 4 (over y, core).
Axes of the slice: x: 2, y: 2, z: 4, core: 2. Of those that a mesh axis runs over, the one named last changes fastest.
Arguments:
- particles: float32 [32, 2, 2, 128, 128], P(('px', 'py')), may hold values from -11 to 11
- orientation: int32 [32], P(('px', 'py')), may hold values from 0 to 7
- wedge_index: int32 [32], P(('px', 'py')), may hold values from 0 to 3
- half_set: int32 [32], P(('px', 'py')), may hold values from 0 to 1
- shell_map: int32 [2, 256, 256], P(None, ('px', 'py')), may hold values from 0 to 31, as said below
Outputs:
- half_maps: float32 [2, 2, 2, 256, 256], P(None, None, None, ('px', 'py'))
- fsc: float32 [32], replicated
Inputs may be any that keep to these rules, and one draw needn't show every extreme that they name: `shell_map`: every shell number occurs in every draw.
All inputs are finite; a program needn't handle non-finite values.
Results may differ from a plain program's by a relative error of at most 0.0003.
Values sent between devices are 32-bit elements; how exact they have to be, the bound alone decides.
No kernel may reach another device: no remote copies, remote signals or barrier semaphores. Data moves between devices by JAX's collectives and lax.ppermute only.
A program may use at most 64 MiB of HBM per device.

v0:
```python
import math
import jax
import jax.numpy as jnp
from jax import lax
from jax.sharding import PartitionSpec as P

NSHELL = 32
wedge_rise = (1, 3, 2, 3)
wedge_run = (1, 2, 1, 1)
sign_first = (1.0, -1.0, -1.0, 1.0, 1.0, -1.0, -1.0, 1.0)
sign_second = (1.0, 1.0, -1.0, -1.0, -1.0, -1.0, 1.0, 1.0)
highest = lax.Precision.HIGHEST


def select(lookup, position):
    entries = jnp.array(lookup)
    return jnp.sum(jnp.where(jnp.arange(len(lookup)) == position, entries, jnp.zeros_like(entries)))


def angle_table(sources, targets, extent):
    phases = sources[:, None] * targets[None, :] % extent
    angles = phases.astype(jnp.float32) * (2.0 * math.pi / extent)
    factor = 1.0 / math.sqrt(extent)
    return (jnp.cos(angles) * factor, jnp.sin(angles) * factor)


def coverage(plane_abs, spectral_abs, wedge_id):
    rise_value = select(wedge_rise, wedge_id)
    run_value = select(wedge_run, wedge_id)
    return (plane_abs[:, None] * run_value <= spectral_abs[None, :] * rise_value).astype(
        jnp.float32
    )


def shards(particles, orientation, wedge_index, half_set, shell_map):
    planes = particles.shape[2]
    box_side = particles.shape[3]
    extent = shell_map.shape[2]
    own_rows = shell_map.shape[1]
    plane_abs = jnp.abs((jnp.arange(planes, dtype=jnp.int32) - planes // 2) * (extent // planes))
    spectral = jnp.arange(extent, dtype=jnp.int32)
    spectral_abs = jnp.minimum(spectral, extent - spectral)
    cos_fwd, sin_fwd = angle_table(
        jnp.arange(box_side, dtype=jnp.int32) - box_side // 2, spectral, extent
    )
    totals = jnp.zeros((2, 2, planes, extent, extent), jnp.float32)
    source = particles[0]
    turn_index = orientation[0]
    swapped = turn_index % 2 == 1
    source = jnp.where(turn_index >= 4, jnp.roll(jnp.flip(source, 1), 1, 1), source)
    source = jnp.where(swapped, jnp.swapaxes(source, 2, 3), source)
    sign_outer = select(sign_first, turn_index)
    sign_inner = select(sign_second, turn_index)
    along_cos = jnp.einsum("czab,bk->czak", source, cos_fwd, precision=highest)
    along_sin = jnp.einsum("czab,bk->czak", source, sin_fwd, precision=highest)
    partial_turn = jnp.stack(
        [along_cos[0] + sign_inner * along_sin[1], along_cos[1] - sign_inner * along_sin[0]]
    )
    outer_cos = jnp.einsum("czak,aj->czjk", partial_turn, cos_fwd, precision=highest)
    outer_sin = jnp.einsum("czak,aj->czjk", partial_turn, sin_fwd, precision=highest)
    spectrum = jnp.stack(
        [outer_cos[0] + sign_outer * outer_sin[1], outer_cos[1] - sign_outer * outer_sin[0]]
    )
    covered = coverage(plane_abs, spectral_abs, wedge_index[0])
    covered = jnp.where(swapped, covered[:, None, :], covered[:, :, None])
    half_id = half_set[0]
    current = lax.dynamic_index_in_dim(totals, half_id, 0, False)
    totals = lax.dynamic_update_index_in_dim(totals, current + spectrum * covered, half_id, 0)
    reduced = lax.psum_scatter(totals, ("px", "py"), scatter_dimension=3, tiled=True)
    half_hot = (half_set[:, None] == jnp.arange(2)).astype(jnp.float32)
    wedge_hot = (wedge_index[:, None] == jnp.arange(4)).astype(jnp.float32)
    parity_hot = (orientation[:, None] % 2 == jnp.arange(2)).astype(jnp.float32)
    local_counts = jnp.einsum("ph,pw,pq->hwq", half_hot, wedge_hot, parity_hot, precision=highest)
    class_totals = lax.psum(local_counts, ("px", "py"))
    row_abs = lax.dynamic_slice_in_dim(
        spectral_abs, lax.axis_index(("px", "py")) * own_rows, own_rows
    )
    row_cover = jnp.stack([coverage(plane_abs, row_abs, wedge_id) for wedge_id in range(4)])
    column_cover = jnp.stack([coverage(plane_abs, spectral_abs, wedge_id) for wedge_id in range(4)])
    by_rows = jnp.einsum("hw,wzt->hzt", class_totals[:, :, 0], row_cover, precision=highest)
    by_columns = jnp.einsum("hw,wzk->hzk", class_totals[:, :, 1], column_cover, precision=highest)
    cover = by_rows[:, :, :, None] + by_columns[:, :, None, :]
    average = reduced / jnp.maximum(cover, 1.0)[:, None]
    cross = average[0, 0] * average[1, 0] + average[0, 1] * average[1, 1]
    power_first = average[0, 0] * average[0, 0] + average[0, 1] * average[0, 1]
    power_second = average[1, 0] * average[1, 0] + average[1, 1] * average[1, 1]
    stacked = jnp.stack([cross, power_first, power_second]).reshape(3, -1)
    membership = (shell_map.reshape(-1)[:, None] == jnp.arange(NSHELL)).astype(jnp.float32)
    shell_part = jnp.dot(stacked, membership, precision=highest)
    shell_total = lax.psum(shell_part, ("px", "py"))
    fsc = shell_total[0] / (jnp.sqrt(shell_total[1] * shell_total[2]) + 1e-06)
    n_rows = lax.axis_size("px")
    n_columns = lax.axis_size("py")
    cos_y, sin_y = angle_table(spectral, spectral, extent)
    middle_cos = jnp.einsum("hcztk,kp->hczpt", average, cos_y, precision=highest)
    middle_sin = jnp.einsum("hcztk,kp->hczpt", average, sin_y, precision=highest)
    middle = jnp.stack(
        [middle_cos[:, 0] - middle_sin[:, 1], middle_sin[:, 0] + middle_cos[:, 1]], axis=1
    )
    arrived = lax.all_to_all(
        lax.all_to_all(middle, "px", split_axis=3, concat_axis=4, tiled=True),
        "py",
        split_axis=3,
        concat_axis=4,
        tiled=True,
    )
    x_slot = spectral // own_rows
    x_source = (x_slot % n_rows * n_columns + x_slot // n_rows) * own_rows + spectral % own_rows
    cos_x, sin_x = angle_table(x_source, spectral, extent)
    final_cos = jnp.einsum("hczym,mx->hczyx", arrived, cos_x, precision=highest)
    final_sin = jnp.einsum("hczym,mx->hczyx", arrived, sin_x, precision=highest)
    half_maps = jnp.stack(
        [final_cos[:, 0] - final_sin[:, 1], final_sin[:, 0] + final_cos[:, 1]], axis=1
    )
    return (half_maps, fsc)


def solution(mesh):
    placed = (
        P(("px", "py"), None, None, None, None),
        P(("px", "py")),
        P(("px", "py")),
        P(("px", "py")),
        P(None, ("px", "py"), None),
    )
    return jax.shard_map(
        shards,
        mesh=mesh,
        in_specs=placed,
        out_specs=(P(None, None, None, ("px", "py"), None), P()),
        check_vma=False,
    )
```

profile of v0, /device:TPU:0, one launch (start us, length us, event | category | flops | bytes accessed | tf_op | source)
XLA Modules:
  0.0 240.1 jit_solution(11886774212349079399)
XLA Ops:
  7.9 1.1 copy.50
  9.0 2.0 fusion.38
  11.0 2.0 fusion.42
  13.1 0.7 fusion.77
  13.8 0.7 fusion.13
  14.5 1.5 convolution_bitcast_fusion.1
  16.0 1.5 convolution_bitcast_fusion
  18.1 0.8 fusion.81
  19.0 0.7 broadcast_multiply_fusion.5
  19.7 0.7 broadcast_multiply_fusion.14
  21.2 1.6 fusion.4
  22.8 0.2 broadcast_in_dim.22
  23.0 0.9 copy-done.1
  24.0 1.3 copy-done
  25.6 42.0 %psum.14 = f32[2,4,2]{1,0,2:T(2,128)S(1)} all-reduce(f32[2,4,2]{1,0,2:T(2,128)S(1)} %multiply_bitcast_fusion), channel_id=1, replica_groups=mesh['px'=8,'py'=4] {'px','py'}, use_global_device_ids=true, to_apply=%region_5.6 | all-reduce | flops 16 | bytes 128 | tf_op jit(solution)/shard_map/psum | solution.py:74
  67.6 0.7 broadcast_multiply_fusion.7
  68.2 0.7 broadcast_multiply_fusion.9
  68.9 0.6 broadcast_multiply_fusion.11
  69.5 0.6 broadcast_multiply_fusion.13
  70.2 0.8 broadcast_multiply_fusion.12
  70.9 1.9 broadcast_multiply_fusion.10
  73.3 0.6 broadcast_multiply_fusion
  73.9 0.6 broadcast_multiply_fusion.1
  74.6 0.7 broadcast_multiply_fusion.2
  75.2 0.7 broadcast_multiply_fusion.3
  76.2 0.1 fusion.68
  76.5 89.9 %reduce-scatter.2.cloned.1.call-done = f32[2,2,2,8,256]{4,3,2,1,0:T(8,128)} async-done(((f32[2,2,2,256,256]{4,3,2,1,0:T(8,128)}), f32[2,2,2,8,256]{4,3,2,1,0:T(8,128)}) %reduce-scatter.2.cloned.1.call-update) | async-done | bytes 65552 | tf_op jit(solution)/shard_map/reduce_scatter | solution.py:69
  166.4 0.8 broadcast_divide_fusion
  167.3 1.3 convolution_bitcast_fusion.2
  168.6 1.3 convolution_bitcast_fusion.3
  170.0 0.7 copy.55
  170.7 2.2 reshape.771
  173.0 3.4 %all-to-all-start = ((f32[8,1,2048]{2,1,0:T(1,128)}), f32[8,1,2048]{2,1,0:T(1,128)S(1)}, u32[]{:S(2)}, u32[]{:S(2)}) async-start(f32[8,1,2048]{2,1,0:T(1,128)} %reshape.771), calls=%async_computation.1 | async-start | bytes 131072 | tf_op jit(solution)/shard_map/all_to_all | solution.py:101
  176.3 0.4 fusion.5
  176.7 39.8 %psum.15 = f32[3,32]{1,0:T(4,128)S(1)} all-reduce(f32[3,32]{1,0:T(4,128)S(1)} %fusion.5), channel_id=1, replica_groups=mesh['px'=8,'py'=4] {'px','py'}, use_global_device_ids=true, to_apply=%region_22.23 | all-reduce | flops 96 | bytes 768 | tf_op jit(solution)/shard_map/psum | solution.py:90
  216.6 0.6 broadcast.865
  217.2 0.8 reduce
  218.0 1.6 reshape.772
  219.6 0.6 copy.56
  220.2 0.2 copy.57
  220.3 0.8 reshape.773
  221.1 3.5 %all-to-all-start.1 = ((f32[4,1,4096]{2,1,0:T(1,128)}), f32[4,1,4096]{2,1,0:T(1,128)S(1)}, u32[]{:S(2)}, u32[]{:S(2)}) async-start(f32[4,1,4096]{2,1,0:T(1,128)} %reshape.773), calls=%async_computation.2 | async-start | bytes 131072 | tf_op jit(solution)/shard_map/all_to_all | solution.py:100
  224.7 0.5 fusion.91
  225.2 3.6 %all-to-all-done.1 = f32[4,1,4096]{2,1,0:T(1,128)S(1)} async-done(((f32[4,1,4096]{2,1,0:T(1,128)}), f32[4,1,4096]{2,1,0:T(1,128)S(1)}, u32[]{:S(2)}, u32[]{:S(2)}) %all-to-all-start.1) | async-done | bytes 65568 | tf_op jit(solution)/shard_map/all_to_all | solution.py:100
  228.8 0.9 reduce.1
  230.0 1.3 fusion.14
  231.3 1.3 fusion.16
  232.6 0.6 pad_maximum_fusion.4
  (50 shorter events, 1.8 us)
Async XLA Ops:
  7.2 5.9 %copy-start.3 = (f32[8]{0:T(128)S(1)}, f32[8]{0:T(128)}, u32[]{:S(2)}) copy-start(f32[8]{0:T(128)} %constant.153.clone) | copy-start | bytes 100
  7.2 5.9 %copy-start.4 = (f32[8]{0:T(128)S(1)}, f32[8]{0:T(128)}, u32[]{:S(2)}) copy-start(f32[8]{0:T(128)} %constant.154.clone) | copy-start | bytes 100
  7.2 159.2 %reduce-scatter.2.cloned.1.call-start = ((), (), s32[]{:S(2)}) async-start(), calls=%async_computation.3 | async-start | bytes 2162688 | tf_op jit(solution)/shard_map/reduce_scatter | solution.py:69
  13.8 4.3 %copy-start.5 = (s32[4]{0:T(128)S(1)}, s32[4]{0:T(128)}, u32[]{:S(2)}) copy-start(s32[4]{0:T(128)} %constant.155.clone) | copy-start | bytes 52
  13.8 4.3 %copy-start.6 = (s32[4]{0:T(128)S(1)}, s32[4]{0:T(128)}, u32[]{:S(2)}) copy-start(s32[4]{0:T(128)} %constant.156.clone) | copy-start | bytes 52
  22.8 1.0 copy-start.1
  23.9 52.5 %copy-start.2 = (s32[2,8,256]{2,1,0:T(8,128)S(1)}, s32[2,8,256]{2,1,0:T(8,128)}, u32[]{:S(2)}) copy-start(s32[2,8,256]{2,1,0:T(8,128)} %param.29) | copy-start | bytes 49156
  24.0 1.4 copy-start
  173.0 43.6 %all-to-all-start = ((f32[8,1,2048]{2,1,0:T(1,128)}), f32[8,1,2048]{2,1,0:T(1,128)S(1)}, u32[]{:S(2)}, u32[]{:S(2)}) async-start(f32[8,1,2048]{2,1,0:T(1,128)} %reshape.771), calls=%async_computation.1 | async-start | bytes 131072 | tf_op jit(solution)/shard_map/all_to_all | solution.py:101
  221.1 7.7 %all-to-all-start.1 = ((f32[4,1,4096]{2,1,0:T(1,128)}), f32[4,1,4096]{2,1,0:T(1,128)S(1)}, u32[]{:S(2)}, u32[]{:S(2)}) async-start(f32[4,1,4096]{2,1,0:T(1,128)} %reshape.773), calls=%async_computation.2 | async-start | bytes 131072 | tf_op jit(solution)/shard_map/all_to_all | solution.py:100
Sparse Core Ops, SparseCore 0:
  25.5 140.9 reduce-scatter.1
where the time goes:
time: 241 us; the launch traced here: 240 us
  waiting for transfers between devices  93.5 us (39%)
  blocking collectives  81.8 us (34%)
  other arithmetic  18 us (7%)
  between operations  16.4 us (7%)
  matrix products  12.8 us (5%)
  local copies, waits for them, and re-layouts  10.6 us (4%)
  starting transfers between devices  6.93 us (3%)
    reduce_scatter x1, waiting for transfers between devices, shards(): lax.psum_scatter(totals, ('px', 'py'), scatter_dimension=3, tiled=True)  89.9 us
    psum x1, blocking collectives, shards(): class_totals = lax.psum(local_counts, ('px', 'py'))  42 us
    psum x1, blocking collectives, shards(): shell_total = lax.psum(shell_part, ('px', 'py'))  39.8 us
    unnamed x22, local copies, waits for them, and re-layouts  7.03 us
    mul x7, other arithmetic, coverage(): spectral_abs[None, :] * rise_value  6 us
  transfers between devices with their start and end apart: 3, of which 2 were waited for; matrix products, arithmetic and copies ran while one was open for 4% of the time, Pallas kernels for 0%

commit v1 on v0

--- a/solution.py
+++ b/solution.py
@@ -97,13 +97,11 @@
     middle = jnp.stack(
         [middle_cos[:, 0] - middle_sin[:, 1], middle_sin[:, 0] + middle_cos[:, 1]], axis=1
     )
-    arrived = lax.all_to_all(
-        lax.all_to_all(middle, "px", split_axis=3, concat_axis=4, tiled=True),
-        "py",
-        split_axis=3,
-        concat_axis=4,
-        tiled=True,
-    )
+    x = lax.all_to_all(middle, "px", split_axis=3, concat_axis=4, tiled=True)
+    peers = lax.axis_size("py")
+    parts = jnp.stack(jnp.split(x, peers, axis=3), axis=0)
+    parts = lax.all_to_all(parts, "py", split_axis=0, concat_axis=0)
+    arrived = jnp.concatenate(parts, axis=4)
     x_slot = spectral // own_rows
     x_source = (x_slot % n_rows * n_columns + x_slot // n_rows) * own_rows + spectral % own_rows
     cos_x, sin_x = angle_table(x_source, spectral, extent)

time: 241 us -> 241 us (level)
  no operation moved by 1% of the time
where the time goes in v1:
time: 241 us
  waiting for transfers between devices  93.4 us (39%)
  blocking collectives  81.9 us (34%)
  other arithmetic  18.1 us (8%)
  between operations  16.4 us (7%)
  matrix products  12.8 us (5%)
  local copies, waits for them, and re-layouts  11.2 us (5%)
  starting transfers between devices  6.93 us (3%)
    reduce_scatter x1, waiting for transfers between devices, shards(): lax.psum_scatter(totals, ('px', 'py'), scatter_dimension=3, tiled=True)  89.8 us
    psum x1, blocking collectives, shards(): class_totals = lax.psum(local_counts, ('px', 'py'))  42 us
    psum x1, blocking collectives, shards(): shell_total = lax.psum(shell_part, ('px', 'py'))  39.9 us
    unnamed x22, local copies, waits for them, and re-layouts  7 us
    mul x7, other arithmetic, coverage(): spectral_abs[None, :] * rise_value  6 us
  transfers between devices with their start and end apart: 3, of which 2 were waited for; matrix products, arithmetic and copies ran while one was open for 4% of the time, Pallas kernels for 0%

profile of v1, /device:TPU:0, one launch (start us, length us, event | category | flops | bytes accessed | tf_op | source)
XLA Modules:
  0.0 240.6 jit_solution(2238187178344235930)
XLA Ops:
  7.9 1.1 copy.54
  9.0 2.0 fusion.38
  11.0 2.0 fusion.42
  13.1 0.7 fusion.77
  13.8 0.7 fusion.13
  14.5 1.5 convolution_bitcast_fusion.1
  16.0 1.5 convolution_bitcast_fusion
  18.1 0.8 fusion.81
  19.0 0.7 broadcast_multiply_fusion.5
  19.7 0.7 broadcast_multiply_fusion.14
  21.2 1.6 fusion.4
  22.8 0.2 broadcast_in_dim.22
  23.0 0.9 copy-done.1
  24.0 1.3 copy-done
  25.6 42.0 %psum.14 = f32[2,4,2]{1,0,2:T(2,128)S(1)} all-reduce(f32[2,4,2]{1,0,2:T(2,128)S(1)} %multiply_bitcast_fusion), channel_id=1, replica_groups=mesh['px'=8,'py'=4] {'px','py'}, use_global_device_ids=true, to_apply=%region_5.6 | all-reduce | flops 16 | bytes 128 | tf_op jit(solution)/shard_map/psum | solution.py:74
  67.6 0.7 broadcast_multiply_fusion.7
  68.3 0.7 broadcast_multiply_fusion.9
  69.0 0.6 broadcast_multiply_fusion.11
  69.5 0.6 broadcast_multiply_fusion.13
  70.2 0.8 broadcast_multiply_fusion.12
  70.9 1.9 broadcast_multiply_fusion.10
  73.3 0.6 broadcast_multiply_fusion
  73.9 0.6 broadcast_multiply_fusion.1
  74.6 0.7 broadcast_multiply_fusion.2
  75.3 0.7 broadcast_multiply_fusion.3
  76.3 0.1 fusion.68
  76.5 89.8 %reduce-scatter.2.cloned.1.call-done = f32[2,2,2,8,256]{4,3,2,1,0:T(8,128)} async-done(((f32[2,2,2,256,256]{4,3,2,1,0:T(8,128)}), f32[2,2,2,8,256]{4,3,2,1,0:T(8,128)}) %reduce-scatter.2.cloned.1.call-update) | async-done | bytes 65552 | tf_op jit(solution)/shard_map/reduce_scatter | solution.py:69
  166.3 0.8 broadcast_divide_fusion
  167.2 1.3 convolution_bitcast_fusion.2
  168.5 1.3 convolution_bitcast_fusion.3
  169.9 0.7 copy.59
  170.6 2.2 reshape.779
  172.9 3.4 %all-to-all-start = ((f32[8,1,2048]{2,1,0:T(1,128)}), f32[8,1,2048]{2,1,0:T(1,128)S(1)}, u32[]{:S(2)}, u32[]{:S(2)}) async-start(f32[8,1,2048]{2,1,0:T(1,128)} %reshape.779), calls=%async_computation.1 | async-start | bytes 131072 | tf_op jit(solution)/shard_map/all_to_all | solution.py:100
  176.2 0.4 fusion.5
  176.6 39.9 %psum.15 = f32[3,32]{1,0:T(4,128)S(1)} all-reduce(f32[3,32]{1,0:T(4,128)S(1)} %fusion.5), channel_id=1, replica_groups=mesh['px'=8,'py'=4] {'px','py'}, use_global_device_ids=true, to_apply=%region_22.23 | all-reduce | flops 96 | bytes 768 | tf_op jit(solution)/shard_map/psum | solution.py:90
  216.5 0.6 broadcast.865
  217.1 0.8 reduce
  217.9 1.6 reshape.780
  219.5 0.6 copy.60
  220.1 0.3 slice_bitcast_fusion.3
  220.9 0.8 reshape.781
  221.6 3.5 %all-to-all-start.1 = ((f32[4,1,4096]{2,1,0:T(1,128)}), f32[4,1,4096]{2,1,0:T(1,128)S(1)}, u32[]{:S(2)}, u32[]{:S(2)}) async-start(f32[4,1,4096]{2,1,0:T(1,128)} %reshape.781), calls=%async_computation.2 | async-start | bytes 131072 | tf_op jit(solution)/shard_map/all_to_all | solution.py:103
  225.2 0.5 fusion.91
  225.7 3.6 %all-to-all-done.1 = f32[4,1,4096]{2,1,0:T(1,128)S(1)} async-done(((f32[4,1,4096]{2,1,0:T(1,128)}), f32[4,1,4096]{2,1,0:T(1,128)S(1)}, u32[]{:S(2)}, u32[]{:S(2)}) %all-to-all-start.1) | async-done | bytes 65568 | tf_op jit(solution)/shard_map/all_to_all | solution.py:103
  229.3 0.9 reduce.1
  230.5 1.3 fusion.14
  231.8 1.3 fusion.16
  233.1 0.6 pad_maximum_fusion.5
  (54 shorter events, 2.3 us)
Async XLA Ops:
  7.2 5.9 %copy-start.3 = (f32[8]{0:T(128)S(1)}, f32[8]{0:T(128)}, u32[]{:S(2)}) copy-start(f32[8]{0:T(128)} %constant.153.clone) | copy-start | bytes 100
  7.2 5.9 %copy-start.4 = (f32[8]{0:T(128)S(1)}, f32[8]{0:T(128)}, u32[]{:S(2)}) copy-start(f32[8]{0:T(128)} %constant.154.clone) | copy-start | bytes 100
  7.2 159.1 %reduce-scatter.2.cloned.1.call-start = ((), (), s32[]{:S(2)}) async-start(), calls=%async_computation.3 | async-start | bytes 2162688 | tf_op jit(solution)/shard_map/reduce_scatter | solution.py:69
  13.8 4.3 %copy-start.5 = (s32[4]{0:T(128)S(1)}, s32[4]{0:T(128)}, u32[]{:S(2)}) copy-start(s32[4]{0:T(128)} %constant.155.clone) | copy-start | bytes 52
  13.8 4.3 %copy-start.6 = (s32[4]{0:T(128)S(1)}, s32[4]{0:T(128)}, u32[]{:S(2)}) copy-start(s32[4]{0:T(128)} %constant.156.clone) | copy-start | bytes 52
  22.8 1.0 copy-start.1
  23.9 52.5 %copy-start.2 = (s32[2,8,256]{2,1,0:T(8,128)S(1)}, s32[2,8,256]{2,1,0:T(8,128)}, u32[]{:S(2)}) copy-start(s32[2,8,256]{2,1,0:T(8,128)} %param.29) | copy-start | bytes 49156
  24.0 1.4 copy-start
  172.9 43.6 %all-to-all-start = ((f32[8,1,2048]{2,1,0:T(1,128)}), f32[8,1,2048]{2,1,0:T(1,128)S(1)}, u32[]{:S(2)}, u32[]{:S(2)}) async-start(f32[8,1,2048]{2,1,0:T(1,128)} %reshape.779), calls=%async_computation.1 | async-start | bytes 131072 | tf_op jit(solution)/shard_map/all_to_all | solution.py:100
  221.6 7.7 %all-to-all-start.1 = ((f32[4,1,4096]{2,1,0:T(1,128)}), f32[4,1,4096]{2,1,0:T(1,128)S(1)}, u32[]{:S(2)}, u32[]{:S(2)}) async-start(f32[4,1,4096]{2,1,0:T(1,128)} %reshape.781), calls=%async_computation.2 | async-start | bytes 131072 | tf_op jit(solution)/shard_map/all_to_all | solution.py:103
Sparse Core Ops, SparseCore 0:
  25.5 140.7 reduce-scatter.1
